TPU v7x, 32 devices: a whole 2x2x4 slice. The times are simulated.
32 devices in a mesh: dp: 8 (over z, y), mp: 4 (over x, core).
Axes of the slice: x: 2, y: 2, z: 4, core: 2. Of those that a mesh axis runs over, the one named last changes fastest.
Arguments:
- query: bfloat16 [4096, 4096], P('dp', 'mp'), may hold values from -6 to 6
- passage: bfloat16 [4096, 4096], P('dp', 'mp'), may hold values from -6 to 6
- query_scale: bfloat16 [4096], P('dp'), may hold values from 0.4 to 2.5
- passage_scale: bfloat16 [4096], P('dp'), may hold values from 0.4 to 2.5
- partners: int32 [8, 3], P('dp'), may hold values from 0 to 3, as said below
- counts: int32 [8], replicated, may hold values from 256 to 512, as said below
Outputs:
- loss: float32 [], replicated
- grad_query: bfloat16 [4096, 4096], P('dp', 'mp')
- grad_passage: bfloat16 [4096, 4096], P('dp', 'mp')
Inputs may be any that keep to these rules, and one draw needn't show every extreme that they name: `partners`: each nonzero entry of a row is a distinct distance; block 0 and the last 3 blocks use all 3 slots. `counts`: some block has all 512 rows valid.
All inputs are finite; a program needn't handle non-finite values.
Results may differ from a plain program's by a relative error of at most 0.004.
Values may be sent and summed in bfloat16 or wider, within the bound.
A program may use at most 64 MiB of HBM per device.

v0:
```python
import functools
import math

import jax
import jax.numpy as jnp
from jax import lax
from jax.experimental import pallas as pl
from jax.experimental.pallas import tpu as pltpu
from jax.sharding import PartitionSpec as P

WIN = 3
CHUNKS = 4
GROUP = 32
MESH = pl.DeviceIdType.MESH


def kernel(ndp, nmp, inv, q_ref, p_ref, ps_ref, qs_ref, meta_ref,
           gq_ref, gp_ref, loss_ref,
           pbuf, qbuf, psbuf, raw, inbox, weights, rw_out, rw_in, lsum, lin,
           p_ss, p_rs, q_ss, q_rs, sc_ss, sc_rs, t_ss, t_rs, k_ss, k_rs,
           d_ss, d_rs, g_ss, g_rs, l_ss, l_rs):
    d = lax.axis_index("dp")
    m = lax.axis_index("mp")
    rows, width = q_ref.shape
    share = rows // nmp
    step = rows // CHUNKS

    def at_dp(delta):
        return (lax.rem(d + delta + ndp, ndp), m)

    def at_mp(delta):
        return (d, lax.rem(m + delta, nmp))

    def flip(index, bit):
        return index + bit - 2 * bit * lax.rem(index // bit, 2)

    def rows_of(block):
        return pl.ds(pl.multiple_of(block * share, share), share)

    even = lax.rem(d, 2) == 0
    odd = lax.rem(d, 2) == 1
    partner = (flip(d, 1), m)
    mp_bits = [1 << b for b in range(nmp.bit_length() - 1)]
    dp_bits = [1 << b for b in range(ndp.bit_length() - 1)]

    peers = [at_dp(s * k) for k in range(1, WIN + 1) for s in (1, -1)]
    peers += [at_mp(j) for j in range(1, nmp)]
    peers += [(flip(d, b), m) for b in dp_bits if b > WIN]
    barrier = pltpu.get_barrier_semaphore()
    for peer in peers:
        pl.semaphore_signal(barrier, inc=1, device_id=peer, device_id_type=MESH)
    pl.semaphore_wait(barrier, len(peers))

    def copy(src, dst, ssem, rsem, dev):
        return pltpu.make_async_remote_copy(
            src_ref=src, dst_ref=dst, send_sem=ssem, recv_sem=rsem,
            device_id=dev, device_id_type=MESH)

    class Stream:
        def __init__(self, own, buf, ss, rs, dest):
            self.own, self.buf, self.ss, self.rs, self.dest = own, buf, ss, rs, dest

        def cut(self, c):
            return pl.ds(c * step, step)

        def direct(self, c):
            s = self.cut(c)
            return copy(self.own.at[s], self.buf.at[1, s], self.ss.at[0, c], self.rs.at[1, c], self.dest)

        def near_relay(self, c):
            s = self.cut(c)
            return copy(self.buf.at[1, s], self.buf.at[0, s], self.ss.at[1, c], self.rs.at[0, c], partner)

        def near_own(self, c):
            s = self.cut(c)
            return copy(self.own.at[s], self.buf.at[0, s], self.ss.at[1, c], self.rs.at[0, c], partner)

        def far_near(self, c):
            s = self.cut(c)
            return copy(self.buf.at[1, s], self.buf.at[2, s], self.ss.at[2, c], self.rs.at[2, c], partner)

        def far_next(self, c):
            s = self.cut(c)
            return copy(self.buf.at[0, s], self.buf.at[2, s], self.ss.at[3, c], self.rs.at[2, c], self.dest)

        def arrived(self, slot, c):
            s = self.cut(c)
            copy(self.buf.at[slot, s], self.buf.at[slot, s], self.ss.at[0, c], self.rs.at[slot, c], partner).wait_recv()

        def start_own(self, is_b):
            for c in range(CHUNKS):
                self.direct(c).start()

            @pl.when(is_b)
            def _():
                for c in range(CHUNKS):
                    self.near_own(c).start()

        def relay_two(self, is_b):
            for c in range(CHUNKS):
                self.arrived(1, c)

                @pl.when(is_b)
                def _():
                    self.far_near(c).start()

                @pl.when(jnp.logical_not(is_b))
                def _():
                    self.near_relay(c).start()

        def relay_one(self, is_b):
            for c in range(CHUNKS):
                self.arrived(0, c)

                @pl.when(is_b)
                def _():
                    self.far_next(c).start()

        def relay_all(self, is_b):
            for c in range(CHUNKS):
                self.arrived(1, c)

                @pl.when(is_b)
                def _():
                    self.far_near(c).start()
                    self.arrived(0, c)
                    self.far_next(c).start()

                @pl.when(jnp.logical_not(is_b))
                def _():
                    self.near_relay(c).start()
                    self.arrived(0, c)

        def finish(self, is_b):
            for c in range(CHUNKS):
                self.direct(c).wait_send()

                @pl.when(is_b)
                def _():
                    self.near_own(c).wait_send()
                    self.far_near(c).wait_send()
                    self.far_next(c).wait_send()

                @pl.when(jnp.logical_not(is_b))
                def _():
                    self.near_relay(c).wait_send()

    ps = Stream(p_ref, pbuf, p_ss, p_rs, at_dp(-2))
    qs = Stream(q_ref, qbuf, q_ss, q_rs, at_dp(2))

    def scale_copy(k):
        return copy(ps_ref, psbuf.at[k - 1], sc_ss.at[k - 1], sc_rs.at[k - 1], at_dp(-k))

    for k in range(1, WIN + 1):
        scale_copy(k).start()
    ps.start_own(odd)

    def across(s):
        block = m
        for b in mp_bits:
            if s & b:
                block = flip(block, b)
        return rows_of(block)

    def tile_copy(k, s):
        return copy(raw.at[k, across(s)], inbox.at[s - 1, k],
                    t_ss.at[s - 1, k], t_rs.at[s - 1, k], (d, flip(m, s & -s)))

    def tile_next(k):
        for bit in mp_bits[1:]:
            for s in range(bit, nmp, 2 * bit):
                for b in mp_bits:
                    if b < bit:
                        tile_copy(k, s | b).wait_recv()
                        raw[k, across(s), :] += inbox[(s | b) - 1, k]
                tile_copy(k, s).start()

    def tile(k):
        keys = p_ref if k == 0 else pbuf.at[k - 1]

        @pl.loop(0, nmp)
        def _(r):
            at = rows_of(r)
            raw[k, at, :] = lax.dot_general(
                q_ref[at, :], keys[...], (((1,), (1,)), ((), ())),
                preferred_element_type=jnp.float32)
        for s in range(1, nmp, 2):
            tile_copy(k, s).start()

    tile(0)
    tile_next(0)
    ps.relay_two(odd)
    qs.start_own(even)
    ps.relay_one(odd)
    tile(2)
    tile(1)
    tile_next(2)
    tile_next(1)
    qs.relay_two(even)
    for c in range(CHUNKS):
        ps.arrived(2, c)
    tile(3)
    tile_next(3)
    for k in range(1, WIN + 1):
        scale_copy(k).wait_recv()
    for k in (0, 2, 1, 3):
        for b in mp_bits:
            tile_copy(k, b).wait_recv()

    lsum[...] = jnp.zeros_like(lsum)

    @pl.loop(0, share // GROUP)
    def _(g):
        low = pl.multiple_of(g * GROUP, GROUP)
        here = pl.ds(low, GROUP)
        whole = pl.ds(pl.multiple_of(m * share + low, GROUP), GROUP)
        row_scale = qs_ref[whole, :]
        cols = lax.broadcasted_iota(jnp.int32, (GROUP, rows), 1)
        ids = lax.broadcasted_iota(jnp.int32, (GROUP, rows), 0) + (m * share + low)
        diagonal = cols == ids
        valid = ids[:, 0:1] < meta_ref[0]
        key_scale = [ps_ref[0:1, :]] + [psbuf[k, 0:1, :] for k in range(WIN)]
        scores = []
        for k in range(WIN + 1):
            s = raw[k, whole, :]
            for b in mp_bits:
                s = s + inbox[b - 1, k, here, :]
            scores.append(s * (row_scale * inv) * key_scale[k])
        masked = [jnp.where(cols < meta_ref[k], scores[k], -jnp.inf) for k in range(WIN + 1)]
        top = functools.reduce(jnp.maximum, [jnp.max(x, axis=1, keepdims=True) for x in masked])
        exps = [jnp.exp(x - top) for x in masked]
        total = sum(jnp.sum(x, axis=1, keepdims=True) for x in exps)
        lse = top + jnp.log(total)
        positive = jnp.sum(jnp.where(diagonal, scores[0], 0.0), axis=1, keepdims=True)
        lost = jnp.sum(jnp.where(valid, lse - positive, 0.0), axis=0, keepdims=True)
        lsum[0] = lsum[0] + lost
        for k in range(WIN + 1):
            grad = exps[k] / total
            if k == 0:
                grad = grad - diagonal.astype(jnp.float32)
            grad = jnp.where(valid, grad, 0.0)
            weights[k, whole, :] = (grad * key_scale[k]).astype(jnp.bfloat16)
            if k == 0:
                weights[WIN + 1, whole, :] = (grad * row_scale).astype(jnp.bfloat16)
            else:
                rw_out[k - 1, here, :] = (grad * row_scale).astype(jnp.bfloat16)

    def dispatch(k):
        return copy(rw_out.at[k - 1], rw_in.at[k - 1, rows_of(m)], d_ss.at[k - 1], d_rs.at[k - 1], at_dp(k))

    for k in range(1, WIN + 1):
        dispatch(k).start()

    class Gather:
        def __init__(self, buf, ss, rs):
            self.buf, self.ss, self.rs = buf, ss, rs
            known = [0]
            self.steps = []
            for bit in reversed(mp_bits):
                self.steps += [(s, bit) for s in known]
                known = known + [s ^ bit for s in known]
            self.steps.sort(key=lambda t: t[0])
            self.got = set()

        def hop(self, s, bit):
            block = m
            for b in mp_bits:
                if s & b:
                    block = flip(block, b)
            part = self.buf.at[:, rows_of(block)]
            return copy(part, part, self.ss.at[s ^ bit], self.rs.at[s ^ bit], (d, flip(m, bit)))

        def take(self, s):
            if s and s not in self.got:
                self.got.add(s)
                block = m
                for b in mp_bits:
                    if s & b:
                        block = flip(block, b)
                part = self.buf.at[:, rows_of(block)]
                copy(part, part, self.ss.at[s], self.rs.at[s], (d, flip(m, 1))).wait_recv()

        def begin(self):
            for s, bit in self.steps:
                if s == 0:
                    self.hop(s, bit).start()

        def rest(self):
            for s, bit in self.steps:
                if s:
                    self.take(s)
                    self.hop(s, bit).start()

        def all(self):
            for s in range(1, nmp):
                self.take(s)

        def finish(self):
            for s, bit in self.steps:
                self.hop(s, bit).wait_send()

    local = Gather(weights, k_ss, k_rs)
    foreign = Gather(rw_in, g_ss, g_rs)
    stages = [(d, flip(m, b)) for b in mp_bits] + [(flip(d, b), m) for b in dp_bits]

    def loss_copy(i):
        return copy(lsum.at[i], lin.at[i], l_ss.at[i], l_rs.at[i], stages[i])

    def loss_step(i):
        if i:
            loss_copy(i - 1).wait_recv()
            lsum[i] = lsum[i - 1] + lin[i - 1]
        if i < len(stages):
            loss_copy(i).start()

    local.begin()
    loss_step(0)
    qs.relay_one(even)
    loss_step(1)
    for k in range(1, WIN + 1):
        dispatch(k).wait_recv()
    foreign.begin()
    loss_step(2)
    local.rest()
    loss_step(3)
    local.all()

    @pl.loop(0, nmp)
    def _(r):
        at = rows_of(r)
        out = jnp.dot(weights[0, at, :], p_ref[...], preferred_element_type=jnp.float32)
        for k in range(WIN):
            out = out + jnp.dot(weights[k + 1, at, :], pbuf[k], preferred_element_type=jnp.float32)
        gq_ref[at, :] = out.astype(jnp.bfloat16)

    loss_step(4)
    foreign.rest()
    def back(w, x):
        return lax.dot_general(w, x, (((0,), (0,)), ((), ())), preferred_element_type=jnp.float32)

    for c in range(CHUNKS):
        qs.arrived(2, c)
    foreign.all()
    for i in range(5, len(stages) + 1):
        loss_step(i)
    loss_ref[...] = lsum[len(stages), 0:1, 0:1] / meta_ref[WIN + 1].astype(jnp.float32)
    jc = 128

    @pl.loop(0, rows // jc)
    def _(t):
        at = pl.ds(pl.multiple_of(t * jc, jc), jc)
        out = back(weights[WIN + 1, :, at], q_ref[...])
        for k in range(WIN):
            out = out + back(rw_in[k, :, at], qbuf[k])
        gp_ref[at, :] = out.astype(jnp.bfloat16)

    ps.finish(odd)
    qs.finish(even)
    for k in range(1, WIN + 1):
        scale_copy(k).wait_send()
        dispatch(k).wait_send()
    for k in range(WIN + 1):
        for j in range(1, nmp):
            tile_copy(k, j).wait_send()
    local.finish()
    foreign.finish()
    for i in range(len(stages)):
        loss_copy(i).wait_send()


def local(ndp, nmp, query, passage, query_scale, passage_scale, partners, counts):
    rows, width = query.shape
    inv = 1.0 / math.sqrt(width * nmp)
    share = rows // nmp
    mine = lax.axis_index("dp")
    ids = jnp.arange(counts.shape[0], dtype=jnp.int32)
    offsets = jnp.arange(WIN + 1, dtype=jnp.int32)
    near = (mine + offsets) % ndp
    key_counts = jnp.sum(jnp.where(ids[None, :] == near[:, None], counts[None, :], 0), axis=1)
    live = (offsets == 0) | jnp.any(partners[0][None, :] == offsets[:, None], axis=1)
    meta = jnp.concatenate([jnp.where(live, key_counts, 0), jnp.sum(counts)[None]]).astype(jnp.int32)
    ps = jnp.broadcast_to(passage_scale.astype(jnp.float32)[None, :], (8, rows))
    qs = query_scale.astype(jnp.float32)[:, None]
    nst = (ndp * nmp).bit_length() - 1
    bf, f32 = jnp.bfloat16, jnp.float32
    dma = pltpu.SemaphoreType.DMA
    vm = pl.BlockSpec(memory_space=pltpu.VMEM)
    gq, gp, loss = pl.pallas_call(
        functools.partial(kernel, ndp, nmp, inv),
        out_shape=[
            jax.ShapeDtypeStruct((rows, width), bf),
            jax.ShapeDtypeStruct((rows, width), bf),
            jax.ShapeDtypeStruct((1, 1), f32),
        ],
        in_specs=[vm] * 4 + [pl.BlockSpec(memory_space=pltpu.SMEM)],
        out_specs=[vm] * 3,
        scratch_shapes=[
            pltpu.VMEM((WIN, rows, width), bf),
            pltpu.VMEM((WIN, rows, width), bf),
            pltpu.VMEM((WIN, 8, rows), f32),
            pltpu.VMEM((WIN + 1, rows, rows), f32),
            pltpu.VMEM((nmp - 1, WIN + 1, share, rows), f32),
            pltpu.VMEM((WIN + 2, rows, rows), bf),
            pltpu.VMEM((WIN, share, rows), bf),
            pltpu.VMEM((WIN, rows, rows), bf),
            pltpu.VMEM((nst + 1, 8, 128), f32),
            pltpu.VMEM((nst, 8, 128), f32),
            dma((4, CHUNKS)), dma((WIN, CHUNKS)),
            dma((4, CHUNKS)), dma((WIN, CHUNKS)),
            dma((WIN,)), dma((WIN,)),
            dma((nmp - 1, WIN + 1)), dma((nmp - 1, WIN + 1)),
            dma((nmp,)), dma((nmp,)),
            dma((WIN,)), dma((WIN,)),
            dma((nmp,)), dma((nmp,)),
            dma((nst,)), dma((nst,)),
        ],
        compiler_params=pltpu.CompilerParams(
            collective_id=0, has_side_effects=True, vmem_limit_bytes=56 * 1024 * 1024),
    )(query, passage, ps, qs, meta)
    return loss.reshape(()), gq, gp


def solution(mesh):
    return jax.shard_map(
        functools.partial(local, mesh.shape["dp"], mesh.shape["mp"]),
        mesh=mesh,
        in_specs=(P("dp", "mp"), P("dp", "mp"), P("dp"), P("dp"), P("dp", None), P()),
        out_specs=(P(), P("dp", "mp"), P("dp", "mp")),
        check_vma=False,
    )
```

profile of v0, /device:TPU:0, one launch (start us, length us, event | category | flops | bytes accessed | tf_op | source)
XLA Modules:
  0.0 131.5 jit_solution(18408923796635732509)
XLA Ops:
  0.6 0.0 copy-start.3
  0.6 0.6 copy-done.3
  1.3 0.6 reduce_sum.19
  1.9 0.2 select_reduce_fusion
  2.1 0.0 copy-start.4
  2.1 0.7 copy-done.4
  2.8 0.1 fusion
  2.9 0.0 copy-start.1
  2.9 1.2 pad_add_fusion.meta_ref
  4.2 0.0 copy-done.1
  4.2 0.0 copy-start.2
  4.2 0.7 copy-done.2
  4.8 0.6 broadcast_in_dim.32.ps_ref
  5.5 0.9 copy.10.qs_ref
  6.3 120.1 %shard_map.85 = (bf16[512,1024]{1,0:T(8,128)(2,1)}, bf16[512,1024]{1,0:T(8,128)(2,1)}, f32[1,1]{1,0:T(1,128)}) custom-call(bf16[512,1024]{1,0:T(8,128)(2,1)} %q_ref.1, bf16[512,1024]{1,0:T(8,128)(2,1)} %p_ref.1, f32[8,512]{1,0:T(8,128)} %broadcast_in_dim.32.ps_ref, f32[512,1]{1,0:T(8,128)} %copy.10.qs_ref, s32[5]{0:T(128)} %pad_add_fusion.meta_ref), custom_call_target="tpu_custom_call" | custom-call | tf_op jit(solution)/shard_map/pallas_call | solution.py:388
  127.0 0.0 copy-start
  127.0 2.4 %copy.15 = bf16[512,1024]{1,0:T(8,128)(2,1)} copy(bf16[512,1024]{1,0:T(8,128)(2,1)} %get-tuple-element.13) | data formatting | bytes 2097152
  129.4 0.0 copy-done
  129.4 1.0 copy.16
  (3 shorter events, 0.0 us)
Async XLA Ops:
  0.6 0.7 copy-start.3
  2.1 0.7 copy-start.4
  2.9 1.3 copy-start.1
  4.2 0.7 copy-start.2
  127.0 2.4 %copy-start = (bf16[512,1024]{1,0:T(8,128)(2,1)S(1)}, bf16[512,1024]{1,0:T(8,128)(2,1)}, u32[]{:S(2)}) copy-start(bf16[512,1024]{1,0:T(8,128)(2,1)} %get-tuple-element.14) | copy-start | bytes 3145732
where the time goes:
time: 132 us; the launch traced here: 131 us
  Pallas kernels  120 us (91%)
  local copies, waits for them, and re-layouts  6.78 us (5%)
  between operations  2.41 us (2%)
  other arithmetic  2.2 us (2%)
    pallas_call x1, Pallas kernels, local(): pl.pallas_call(functools.partial(kernel, ndp, nmp, inv), out_shape=[jax.S...  120 us
    unnamed x12, local copies, waits for them, and re-layouts  5.31 us

commit v1 on v0

v1 whole, which is shorter than its diff:
```python
import functools
import math

import jax
import jax.numpy as jnp
from jax import lax
from jax.experimental import pallas as pl
from jax.experimental.pallas import tpu as pltpu
from jax.sharding import PartitionSpec as P

WIN = 3
CHUNKS = 8
GROUP = 32
MESH = pl.DeviceIdType.MESH
ROWS_BY_ROWS = (((1,), (1,)), ((), ()))
COLS_BY_ROWS = (((0,), (0,)), ((), ()))


def kernel(ndp, nmp, inv, q_hbm, p_hbm, ps_ref, qs_ref, partners_ref, counts_ref,
           gq_ref, gp_ref, loss_ref,
           q_ref, p_ref, pbuf, qbuf, psown, psbuf, raw, inbox, weights, rw_out, rw_in, acc, lsum, lin,
           own_sem, p_ss, p_rs, q_ss, q_rs, sc_ss, sc_rs, t_ss, t_rs, k_ss, k_rs,
           d_ss, d_rs, g_ss, g_rs, l_ss, l_rs):
    d = lax.axis_index("dp")
    m = lax.axis_index("mp")
    rows, width = q_ref.shape
    share = rows // nmp
    step = rows // CHUNKS
    half = rows // 2
    first = CHUNKS // 2

    def at_dp(delta):
        return (lax.rem(d + delta + ndp, ndp), m)

    def flip(index, bit):
        return index + bit - 2 * bit * lax.rem(index // bit, 2)

    def rows_of(block):
        return pl.ds(pl.multiple_of(block * share, share), share)

    def half_of(h):
        return pl.ds(pl.multiple_of(h * half, half), half)

    even = lax.rem(d, 2) == 0
    odd = lax.rem(d, 2) == 1
    parity = lax.rem(d, 2)
    partner = (flip(d, 1), m)
    mp_bits = [1 << b for b in range(nmp.bit_length() - 1)]
    dp_bits = [1 << b for b in range(ndp.bit_length() - 1)]

    own_q = pltpu.make_async_copy(q_hbm, q_ref, own_sem.at[0])
    own_p = pltpu.make_async_copy(p_hbm, p_ref, own_sem.at[1])
    own_q.start()
    own_p.start()

    peers = [at_dp(s * k) for k in range(1, WIN + 1) for s in (1, -1)]
    peers += [(d, flip(m, b)) for b in mp_bits]
    peers += [(flip(d, b), m) for b in dp_bits if b > WIN]
    barrier = pltpu.get_barrier_semaphore()
    for peer in peers:
        pl.semaphore_signal(barrier, inc=1, device_id=peer, device_id_type=MESH)
    psown[...] = jnp.broadcast_to(ps_ref[...].astype(jnp.float32), psown.shape)
    pl.semaphore_wait(barrier, len(peers))

    def copy(src, dst, ssem, rsem, dev):
        return pltpu.make_async_remote_copy(
            src_ref=src, dst_ref=dst, send_sem=ssem, recv_sem=rsem,
            device_id=dev, device_id_type=MESH)

    class Stream:
        def __init__(self, own, buf, ss, rs, dest, far):
            self.own, self.buf, self.ss, self.rs, self.dest = own, buf, ss, rs, dest
            self.far, self.near = far, jnp.logical_not(far)

        def cut(self, c):
            return pl.ds(c * step, step)

        def move(self, kind, source, target, c, dev):
            s = self.cut(c)
            src = self.own.at[s] if source is None else self.buf.at[source, s]
            return copy(src, self.buf.at[target, s], self.ss.at[kind, c], self.rs.at[target, c], dev)

        def direct(self, c):
            return self.move(0, None, 1, c, self.dest)

        def across_own(self, c):
            return self.move(1, None, 0, c, partner)

        def across_one(self, c):
            return self.move(1, 1, 0, c, partner)

        def onward(self, c):
            return self.move(2, 0, 2, c, self.dest)

        def across_first(self, c):
            return self.move(3, 1, 2, c, partner)

        def across_second(self, c):
            return self.move(3, 2, 1, c, partner)

        def arrived(self, slot, c):
            s = self.cut(c)
            copy(self.buf.at[slot, s], self.buf.at[slot, s], self.ss.at[0, c], self.rs.at[slot, c], partner).wait_recv()

        def begin(self):
            @pl.when(self.far)
            def _():
                for c in range(CHUNKS):
                    self.across_own(c).start()
                    if c < first:
                        self.direct(c).start()

            @pl.when(self.near)
            def _():
                for c in range(CHUNKS):
                    self.direct(c).start()

        def relay(self, c):
            @pl.when(self.far)
            def _():
                if c < first:
                    self.arrived(1, c)
                    self.across_first(c).start()
                self.arrived(0, c)
                self.onward(c).start()

            @pl.when(self.near)
            def _():
                self.arrived(1, c)
                self.across_one(c).start()
                self.arrived(0, c)
                if c >= first:
                    self.onward(c).start()

        def early(self):
            @pl.when(self.far)
            def _():
                for c in range(first):
                    self.arrived(2, c)

        def relay_late(self, c):
            @pl.when(self.far)
            def _():
                self.arrived(1, c)

            @pl.when(self.near)
            def _():
                self.arrived(2, c)
                self.across_second(c).start()

        def late(self):
            @pl.when(self.far)
            def _():
                for c in range(first, CHUNKS):
                    self.arrived(2, c)

            @pl.when(self.near)
            def _():
                for c in range(first):
                    self.arrived(2, c)

        def finish(self):
            @pl.when(self.far)
            def _():
                for c in range(CHUNKS):
                    self.across_own(c).wait_send()
                    self.onward(c).wait_send()
                    if c < first:
                        self.direct(c).wait_send()
                        self.across_first(c).wait_send()

            @pl.when(self.near)
            def _():
                for c in range(CHUNKS):
                    self.direct(c).wait_send()
                    self.across_one(c).wait_send()
                    if c >= first:
                        self.onward(c).wait_send()
                        self.across_second(c).wait_send()

    ps = Stream(p_hbm, pbuf, p_ss, p_rs, at_dp(-2), odd)
    qs = Stream(q_hbm, qbuf, q_ss, q_rs, at_dp(2), even)

    def scale_copy(k):
        return copy(psown, psbuf.at[k - 1], sc_ss.at[k - 1], sc_rs.at[k - 1], at_dp(-k))

    ps.begin()
    for k in range(1, WIN + 1):
        scale_copy(k).start()

    def across(s):
        block = m
        for b in mp_bits:
            if s & b:
                block = flip(block, b)
        return rows_of(block)

    def tile_copy(k, h, s):
        return copy(raw.at[k, h, across(s)], inbox.at[s - 1, k, h],
                    t_ss.at[s - 1, k, h], t_rs.at[s - 1, k, h], (d, flip(m, s & -s)))

    def tile_next(k, h):
        for bit in mp_bits[1:]:
            for s in range(bit, nmp, 2 * bit):
                for b in mp_bits:
                    if b < bit:
                        tile_copy(k, h, s | b).wait_recv()
                        raw[k, h, across(s), :] += inbox[(s | b) - 1, k, h]
                tile_copy(k, h, s).start()

    def tile(k, h, keys):
        raw[k, h] = lax.dot_general(q_ref[...], keys, ROWS_BY_ROWS, preferred_element_type=jnp.float32)
        for s in range(1, nmp, 2):
            tile_copy(k, h, s).start()

    def tile_far(k, h):
        tile(k, h, pbuf[k - 1, half_of(h), :])

    own_q.wait()
    own_p.wait()
    for h in range(2):
        tile(0, h, p_ref[h * half:(h + 1) * half, :])
    ps.relay(0)
    for h in range(2):
        tile_next(0, h)
    for c in range(1, first):
        ps.relay(c)
    tile_far(2, 0)
    ps.relay(first)
    tile_next(2, 0)
    tile_far(1, 0)
    ps.relay(first + 1)
    tile_next(1, 0)
    for c in range(first + 2, CHUNKS):
        ps.relay(c)
    tile_far(1, 1)
    ps.early()
    tile_far(2 + parity, 1 - parity)
    tile_next(1, 1)
    tile_next(2 + parity, 1 - parity)
    for c in range(first, CHUNKS):
        ps.relay_late(c)
    qs.begin()
    tile_far(3 - parity, 1)
    ps.late()
    tile_far(3, parity)
    tile_next(3 - parity, 1)
    tile_next(3, parity)
    for k in range(1, WIN + 1):
        scale_copy(k).wait_recv()
    qs.relay(0)
    for k in range(WIN + 1):
        for h in range(2):
            for b in mp_bits:
                tile_copy(k, h, b).wait_recv()

    lsum[...] = jnp.zeros_like(lsum)
    live = [None] + [functools.reduce(jnp.logical_or, [partners_ref[0, j] == k for j in range(partners_ref.shape[1])])
                     for k in range(1, WIN + 1)]
    counted = [counts_ref[lax.rem(d + k, ndp)] for k in range(WIN + 1)]
    key_count = [counted[0]] + [jnp.where(live[k], counted[k], 0) for k in range(1, WIN + 1)]
    query_scale = qs_ref[...].astype(jnp.float32)

    @pl.loop(0, share // GROUP)
    def _(g):
        low = pl.multiple_of(g * GROUP, GROUP)
        here = pl.ds(low, GROUP)
        whole = pl.ds(pl.multiple_of(m * share + low, GROUP), GROUP)
        cols = lax.broadcasted_iota(jnp.int32, (GROUP, rows), 1)
        ids = lax.broadcasted_iota(jnp.int32, (GROUP, rows), 0) + (m * share + low)
        diagonal = cols == ids
        row_scale = jnp.sum(jnp.where(diagonal, query_scale, 0.0), axis=1, keepdims=True)
        valid = ids[:, 0:1] < key_count[0]
        key_scale = [psown[0:1, :]] + [psbuf[k, 0:1, :] for k in range(WIN)]
        scores = []
        for k in range(WIN + 1):
            parts = []
            for h in range(2):
                s = raw[k, h, whole, :]
                for b in mp_bits:
                    s = s + inbox[b - 1, k, h, here, :]
                parts.append(s)
            scores.append(jnp.concatenate(parts, axis=1) * (row_scale * inv) * key_scale[k])
        masked = [jnp.where(cols < key_count[k], scores[k], -jnp.inf) for k in range(WIN + 1)]
        top = functools.reduce(jnp.maximum, [jnp.max(x, axis=1, keepdims=True) for x in masked])
        exps = [jnp.exp(x - top) for x in masked]
        total = sum(jnp.sum(x, axis=1, keepdims=True) for x in exps)
        lse = top + jnp.log(total)
        positive = jnp.sum(jnp.where(diagonal, scores[0], 0.0), axis=1, keepdims=True)
        lost = jnp.sum(jnp.where(valid, lse - positive, 0.0), axis=0, keepdims=True)
        lsum[0] = lsum[0] + lost
        for k in range(WIN + 1):
            grad = exps[k] / total
            if k == 0:
                grad = grad - diagonal.astype(jnp.float32)
            grad = jnp.where(valid, grad, 0.0)
            weights[k, whole, :] = (grad * key_scale[k]).astype(jnp.bfloat16)
            if k == 0:
                weights[WIN + 1, whole, :] = (grad * row_scale).astype(jnp.bfloat16)
            else:
                rw_out[k - 1, here, :] = (grad * row_scale).astype(jnp.bfloat16)

    def dispatch(k):
        return copy(rw_out.at[k - 1], rw_in.at[k - 1, rows_of(m)], d_ss.at[k - 1], d_rs.at[k - 1], at_dp(k))

    for k in range(1, WIN + 1):
        dispatch(k).start()

    class Gather:
        def __init__(self, buf, ss, rs):
            self.buf, self.ss, self.rs = buf, ss, rs
            known = [0]
            self.steps = []
            for bit in reversed(mp_bits):
                self.steps += [(s, bit) for s in known]
                known = known + [s ^ bit for s in known]
            self.steps.sort(key=lambda t: t[0])
            self.got = set()

        def hop(self, s, bit):
            part = self.buf.at[:, across(s)]
            return copy(part, part, self.ss.at[s ^ bit], self.rs.at[s ^ bit], (d, flip(m, bit)))

        def take(self, s):
            if s and s not in self.got:
                self.got.add(s)
                part = self.buf.at[:, across(s)]
                copy(part, part, self.ss.at[s], self.rs.at[s], (d, flip(m, 1))).wait_recv()

        def begin(self):
            for s, bit in self.steps:
                if s == 0:
                    self.hop(s, bit).start()

        def rest(self):
            for s, bit in self.steps:
                if s:
                    self.take(s)
                    self.hop(s, bit).start()

        def all(self):
            for s in range(1, nmp):
                self.take(s)

        def finish(self):
            for s, bit in self.steps:
                self.hop(s, bit).wait_send()

    local = Gather(weights, k_ss, k_rs)
    foreign = Gather(rw_in, g_ss, g_rs)
    stages = [(d, flip(m, b)) for b in mp_bits] + [(flip(d, b), m) for b in dp_bits]

    def loss_copy(i):
        return copy(lsum.at[i], lin.at[i], l_ss.at[i], l_rs.at[i], stages[i])

    def loss_step(i):
        if i > len(stages):
            return
        if i:
            loss_copy(i - 1).wait_recv()
            lsum[i] = lsum[i - 1] + lin[i - 1]
        if i < len(stages):
            loss_copy(i).start()

    local.begin()
    loss_step(0)
    for c in range(1, first):
        qs.relay(c)
        loss_step(c)
    for k in range(1, WIN + 1):
        dispatch(k).wait_recv()
    foreign.begin()
    for c in range(first, CHUNKS):
        qs.relay(c)
        loss_step(c)
    local.rest()
    local.all()

    @pl.loop(0, nmp)
    def _(r):
        at = rows_of(r)
        out = jnp.dot(weights[0, at, :], p_ref[...], preferred_element_type=jnp.float32)
        for k in range(WIN):
            out = out + jnp.dot(weights[k + 1, at, :], pbuf[k], preferred_element_type=jnp.float32)
        gq_ref[at, :] = out.astype(jnp.bfloat16)

    foreign.rest()
    foreign.all()
    for i in range(CHUNKS, len(stages) + 1):
        loss_step(i)
    total_count = functools.reduce(lambda x, y: x + y, [counts_ref[i] for i in range(ndp)])
    loss_ref[...] = lsum[len(stages), 0:1, 0:1] / total_count.astype(jnp.float32)

    def back(w, x):
        return lax.dot_general(w, x, COLS_BY_ROWS, preferred_element_type=jnp.float32)

    qs.early()
    far = 1 - parity
    mid = (1 + far, half_of(1 - far))
    late_a = (2 - far, half_of(1))
    late_b = (2, half_of(far))

    for r in range(2):
        at = pl.ds(r * half, half)
        acc[at, :] = (back(weights[WIN + 1, :, at], q_ref[...]) + back(rw_in[0, :, at], qbuf[0])
                      + back(rw_in[1, 0:half, at], qbuf[1, 0:half, :])
                      + back(rw_in[mid[0], mid[1], at], qbuf[mid[0], mid[1], :]))
    for c in range(first, CHUNKS):
        qs.relay_late(c)
    for r in range(2):
        at = pl.ds(r * half, half)
        acc[at, :] = acc[at, :] + back(rw_in[late_a[0], late_a[1], at], qbuf[late_a[0], late_a[1], :])
    qs.late()
    for r in range(2):
        at = pl.ds(r * half, half)
        gp_ref[at, :] = (acc[at, :] + back(rw_in[late_b[0], late_b[1], at], qbuf[late_b[0], late_b[1], :])
                         ).astype(jnp.bfloat16)

    ps.finish()
    qs.finish()
    for k in range(1, WIN + 1):
        scale_copy(k).wait_send()
        dispatch(k).wait_send()
    for k in range(WIN + 1):
        for h in range(2):
            for j in range(1, nmp):
                tile_copy(k, h, j).wait_send()
    local.finish()
    foreign.finish()
    for i in range(len(stages)):
        loss_copy(i).wait_send()


def local(ndp, nmp, query, passage, query_scale, passage_scale, partners, counts):
    rows, width = query.shape
    inv = 1.0 / math.sqrt(width * nmp)
    share = rows // nmp
    nst = (ndp * nmp).bit_length() - 1
    bf, f32 = jnp.bfloat16, jnp.float32
    dma = pltpu.SemaphoreType.DMA
    vm = pl.BlockSpec(memory_space=pltpu.VMEM)
    sm = pl.BlockSpec(memory_space=pltpu.SMEM)
    hbm = pl.BlockSpec(memory_space=pl.ANY)
    gq, gp, loss = pl.pallas_call(
        functools.partial(kernel, ndp, nmp, inv),
        out_shape=[
            jax.ShapeDtypeStruct((rows, width), bf),
            jax.ShapeDtypeStruct((rows, width), bf),
            jax.ShapeDtypeStruct((1, 1), f32),
        ],
        in_specs=[hbm, hbm, vm, vm, sm, sm],
        out_specs=[vm] * 3,
        scratch_shapes=[
            pltpu.VMEM((rows, width), bf),
            pltpu.VMEM((rows, width), bf),
            pltpu.VMEM((WIN, rows, width), bf),
            pltpu.VMEM((WIN, rows, width), bf),
            pltpu.VMEM((8, rows), f32),
            pltpu.VMEM((WIN, 8, rows), f32),
            pltpu.VMEM((WIN + 1, 2, rows, rows // 2), f32),
            pltpu.VMEM((nmp - 1, WIN + 1, 2, share, rows // 2), f32),
            pltpu.VMEM((WIN + 2, rows, rows), bf),
            pltpu.VMEM((WIN, share, rows), bf),
            pltpu.VMEM((WIN, rows, rows), bf),
            pltpu.VMEM((rows, width), f32),
            pltpu.VMEM((nst + 1, 8, 128), f32),
            pltpu.VMEM((nst, 8, 128), f32),
            dma((2,)),
            dma((4, CHUNKS)), dma((WIN, CHUNKS)),
            dma((4, CHUNKS)), dma((WIN, CHUNKS)),
            dma((WIN,)), dma((WIN,)),
            dma((nmp - 1, WIN + 1, 2)), dma((nmp - 1, WIN + 1, 2)),
            dma((nmp,)), dma((nmp,)),
            dma((WIN,)), dma((WIN,)),
            dma((nmp,)), dma((nmp,)),
            dma((nst,)), dma((nst,)),
        ],
        compiler_params=pltpu.CompilerParams(
            collective_id=0, has_side_effects=True, vmem_limit_bytes=48 * 1024 * 1024),
    )(query, passage, passage_scale[None, :], query_scale[None, :], partners, counts)
    return loss.reshape(()), gq, gp


def solution(mesh):
    return jax.shard_map(
        functools.partial(local, mesh.shape["dp"], mesh.shape["mp"]),
        mesh=mesh,
        in_specs=(P("dp", "mp"), P("dp", "mp"), P("dp"), P("dp"), P("dp", None), P()),
        out_specs=(P(), P("dp", "mp"), P("dp", "mp")),
        check_vma=False,
    )
```

time: 132 us -> 124 us (0.939)
  Pallas kernels: 120 us -> 116 us
  other arithmetic: 2.2 us -> 0 us
    pallas_call x1, Pallas kernels: 120 us -> 116 us  [local(): pl.pallas_call(functools.partial(kernel, ndp, nmp, inv), out_shape=[jax.S...]
where the time goes in v1:
time: 124 us
  Pallas kernels  116 us (94%)
  local copies, waits for them, and re-layouts  5.74 us (5%)
  between operations  2.35 us (2%)
    pallas_call x1, Pallas kernels, local(): pl.pallas_call(functools.partial(kernel, ndp, nmp, inv), out_shape=[jax.S...  116 us
    unnamed x12, local copies, waits for them, and re-layouts  5.05 us

profile of v1, /device:TPU:0, one launch (start us, length us, event | category | flops | bytes accessed | tf_op | source)
XLA Modules:
  0.0 124.1 jit_solution(5567363444259178382)
XLA Ops:
  0.6 0.0 copy-start.4
  0.6 0.7 broadcast_in_dim.7.qs_ref
  1.3 0.0 copy-done.4
  1.3 0.0 copy-start.2
  1.3 0.0 copy-start.3
  1.4 0.6 copy-done.2
  2.0 0.0 copy-done.3
  2.0 0.0 copy-start
  2.0 1.2 copy-done
  3.2 0.0 copy-start.1
  3.2 1.2 copy-done.1
  4.5 116.1 %shard_map.85 = (bf16[512,1024]{1,0:T(8,128)(2,1)S(1)}, bf16[512,1024]{1,0:T(8,128)(2,1)S(1)}, f32[1,1]{1,0:T(1,128)}) custom-call(bf16[512,1024]{1,0:T(8,128)(2,1)S(1)} %copy-done, bf16[512,1024]{1,0:T(8,128)(2,1)S(1)} %copy-done.1, bf16[1,512]{1,0:T(2,128)(2,1)S(1)} %broadcast_in_dim.6.ps_ref, bf16[1,512]{1,0:T(2,128)(2,1)S(1)} %broadcast_in_dim.7.qs_ref, ...), custom_call_target="tpu_custom_call" | custom-call | tf_op jit(solution)/shard_map/pallas_call | solution.py:444
  121.1 1.0 copy.13
  122.1 1.0 copy.14
  (1 shorter events, 0.0 us)
Async XLA Ops:
  0.6 0.7 copy-start.4
  1.3 0.7 copy-start.2
  1.3 0.7 copy-start.3
  2.0 1.2 copy-start
  3.2 1.2 copy-start.1

commit v2 on v1

--- a/solution.py
+++ b/solution.py
@@ -10,16 +10,17 @@
 
 WIN = 3
 CHUNKS = 8
+FIRST = 5
 GROUP = 32
 MESH = pl.DeviceIdType.MESH
 ROWS_BY_ROWS = (((1,), (1,)), ((), ()))
 COLS_BY_ROWS = (((0,), (0,)), ((), ()))
 
 
-def kernel(ndp, nmp, inv, q_hbm, p_hbm, ps_ref, qs_ref, partners_ref, counts_ref,
+def kernel(ndp, nmp, inv, q_hbm, p_hbm, ps_hbm, qs_hbm, partners_hbm, counts_hbm,
            gq_ref, gp_ref, loss_ref,
-           q_ref, p_ref, pbuf, qbuf, psown, psbuf, raw, inbox, weights, rw_out, rw_in, acc, lsum, lin,
-           own_sem, p_ss, p_rs, q_ss, q_rs, sc_ss, sc_rs, t_ss, t_rs, k_ss, k_rs,
+           q_ref, p_ref, ps_ref, qs_ref, partners_ref, counts_ref, pbuf, qbuf, psown, psbuf, raw, inbox, weights, rw_out, rw_in, acc, lsum, lin,
+           own_sem, p_ss, p_rs, q_ss, q_rs, t_ss, t_rs, k_ss, k_rs,
            d_ss, d_rs, g_ss, g_rs, l_ss, l_rs):
     d = lax.axis_index("dp")
     m = lax.axis_index("mp")
@@ -27,13 +28,20 @@
     share = rows // nmp
     step = rows // CHUNKS
     half = rows // 2
-    first = CHUNKS // 2
+    first = FIRST
+    middle = CHUNKS // 2
 
     def at_dp(delta):
         return (lax.rem(d + delta + ndp, ndp), m)
 
     def flip(index, bit):
         return index + bit - 2 * bit * lax.rem(index // bit, 2)
+
+    def flip_all(index, bits):
+        for b in (1 << i for i in range(bits.bit_length())):
+            if bits & b:
+                index = flip(index, b)
+        return index
 
     def rows_of(block):
         return pl.ds(pl.multiple_of(block * share, share), share)
@@ -48,18 +56,23 @@
     mp_bits = [1 << b for b in range(nmp.bit_length() - 1)]
     dp_bits = [1 << b for b in range(ndp.bit_length() - 1)]
 
+    small = [(ps_hbm, ps_ref), (qs_hbm, qs_ref), (partners_hbm, partners_ref), (counts_hbm, counts_ref)]
+    small = [pltpu.make_async_copy(src, dst, own_sem.at[2 + i]) for i, (src, dst) in enumerate(small)]
     own_q = pltpu.make_async_copy(q_hbm, q_ref, own_sem.at[0])
     own_p = pltpu.make_async_copy(p_hbm, p_ref, own_sem.at[1])
-    own_q.start()
-    own_p.start()
-
-    peers = [at_dp(s * k) for k in range(1, WIN + 1) for s in (1, -1)]
+
+    peers = [partner, at_dp(2), at_dp(-2)]
     peers += [(d, flip(m, b)) for b in mp_bits]
-    peers += [(flip(d, b), m) for b in dp_bits if b > WIN]
+    peers += [(flip(d, b), m) for b in dp_bits if b > WIN + 1]
     barrier = pltpu.get_barrier_semaphore()
     for peer in peers:
         pl.semaphore_signal(barrier, inc=1, device_id=peer, device_id_type=MESH)
-    psown[...] = jnp.broadcast_to(ps_ref[...].astype(jnp.float32), psown.shape)
+    for c in small:
+        c.start()
+    own_q.start()
+    own_p.start()
+    small[0].wait()
+    psown[...] = jnp.broadcast_to(ps_ref[...].astype(jnp.float32)[None, :], psown.shape)
     pl.semaphore_wait(barrier, len(peers))
 
     def copy(src, dst, ssem, rsem, dev):
@@ -68,17 +81,19 @@
             device_id=dev, device_id_type=MESH)
 
     class Stream:
-        def __init__(self, own, buf, ss, rs, dest, far):
+        def __init__(self, own, buf, ss, rs, dest, far, extra=None):
             self.own, self.buf, self.ss, self.rs, self.dest = own, buf, ss, rs, dest
-            self.far, self.near = far, jnp.logical_not(far)
-
-        def cut(self, c):
-            return pl.ds(c * step, step)
+            self.far, self.near, self.extra = far, jnp.logical_not(far), extra
+            self.order = ([] if extra is None else [-1]) + list(range(CHUNKS))
+
+        def cut(self, slot, c):
+            own, buf = (self.own, self.buf) if c >= 0 else self.extra
+            at = pl.ds(max(c, 0) * step, step if c >= 0 else own.shape[0])
+            return own.at[at] if slot is None else buf.at[slot, at]
 
         def move(self, kind, source, target, c, dev):
-            s = self.cut(c)
-            src = self.own.at[s] if source is None else self.buf.at[source, s]
-            return copy(src, self.buf.at[target, s], self.ss.at[kind, c], self.rs.at[target, c], dev)
+            return copy(self.cut(source, c), self.cut(target, c),
+                        self.ss.at[kind, c % (CHUNKS + 1)], self.rs.at[target, c % (CHUNKS + 1)], dev)
 
         def direct(self, c):
             return self.move(0, None, 1, c, self.dest)
@@ -99,20 +114,19 @@
             return self.move(3, 2, 1, c, partner)
 
         def arrived(self, slot, c):
-            s = self.cut(c)
-            copy(self.buf.at[slot, s], self.buf.at[slot, s], self.ss.at[0, c], self.rs.at[slot, c], partner).wait_recv()
+            self.move(0, slot, slot, c, partner).wait_recv()
 
         def begin(self):
             @pl.when(self.far)
             def _():
-                for c in range(CHUNKS):
+                for c in self.order:
                     self.across_own(c).start()
                     if c < first:
                         self.direct(c).start()
 
             @pl.when(self.near)
             def _():
-                for c in range(CHUNKS):
+                for c in self.order:
                     self.direct(c).start()
 
         def relay(self, c):
@@ -135,7 +149,7 @@
         def early(self):
             @pl.when(self.far)
             def _():
-                for c in range(first):
+                for c in range(middle):
                     self.arrived(2, c)
 
         def relay_late(self, c):
@@ -149,20 +163,29 @@
                 self.across_second(c).start()
 
         def late(self):
+            @pl.when(self.near)
+            def _():
+                for c in range(middle):
+                    self.arrived(2, c)
+
+        def last(self):
             @pl.when(self.far)
             def _():
-                for c in range(first, CHUNKS):
+                for c in range(middle, CHUNKS):
                     self.arrived(2, c)
 
             @pl.when(self.near)
             def _():
-                for c in range(first):
+                for c in range(middle, first):
                     self.arrived(2, c)
+
+        def last_extra(self):
+            self.arrived(2, -1)
 
         def finish(self):
             @pl.when(self.far)
             def _():
-                for c in range(CHUNKS):
+                for c in self.order:
                     self.across_own(c).wait_send()
                     self.onward(c).wait_send()
                     if c < first:
@@ -171,22 +194,17 @@
 
             @pl.when(self.near)
             def _():
-                for c in range(CHUNKS):
+                for c in self.order:
                     self.direct(c).wait_send()
                     self.across_one(c).wait_send()
                     if c >= first:
                         self.onward(c).wait_send()
                         self.across_second(c).wait_send()
 
-    ps = Stream(p_hbm, pbuf, p_ss, p_rs, at_dp(-2), odd)
+    ps = Stream(p_hbm, pbuf, p_ss, p_rs, at_dp(-2), odd, (psown, psbuf))
     qs = Stream(q_hbm, qbuf, q_ss, q_rs, at_dp(2), even)
 
-    def scale_copy(k):
-        return copy(psown, psbuf.at[k - 1], sc_ss.at[k - 1], sc_rs.at[k - 1], at_dp(-k))
-
     ps.begin()
-    for k in range(1, WIN + 1):
-        scale_copy(k).start()
 
     def across(s):
         block = m
@@ -220,18 +238,19 @@
     own_p.wait()
     for h in range(2):
         tile(0, h, p_ref[h * half:(h + 1) * half, :])
+    ps.relay(-1)
     ps.relay(0)
     for h in range(2):
         tile_next(0, h)
-    for c in range(1, first):
+    for c in range(1, middle):
         ps.relay(c)
     tile_far(2, 0)
-    ps.relay(first)
+    ps.relay(middle)
     tile_next(2, 0)
     tile_far(1, 0)
-    ps.relay(first + 1)
+    ps.relay(middle + 1)
     tile_next(1, 0)
-    for c in range(first + 2, CHUNKS):
+    for c in range(middle + 2, CHUNKS):
         ps.relay(c)
     tile_far(1, 1)
     ps.early()
@@ -241,14 +260,16 @@
     for c in range(first, CHUNKS):
         ps.relay_late(c)
     qs.begin()
-    tile_far(3 - parity, 1)
     ps.late()
-    tile_far(3, parity)
-    tile_next(3 - parity, 1)
-    tile_next(3, parity)
-    for k in range(1, WIN + 1):
-        scale_copy(k).wait_recv()
+    tile_far(3 - parity, parity)
+    ps.last()
+    tile_far(3, 1)
+    tile_next(3 - parity, parity)
+    tile_next(3, 1)
+    ps.last_extra()
     qs.relay(0)
+    for c in small[1:]:
+        c.wait()
     for k in range(WIN + 1):
         for h in range(2):
             for b in mp_bits:
@@ -259,7 +280,7 @@
                      for k in range(1, WIN + 1)]
     counted = [counts_ref[lax.rem(d + k, ndp)] for k in range(WIN + 1)]
     key_count = [counted[0]] + [jnp.where(live[k], counted[k], 0) for k in range(1, WIN + 1)]
-    query_scale = qs_ref[...].astype(jnp.float32)
+    query_scale = qs_ref[...].astype(jnp.float32)[None, :]
 
     @pl.loop(0, share // GROUP)
     def _(g):
@@ -348,32 +369,33 @@
 
     local = Gather(weights, k_ss, k_rs)
     foreign = Gather(rw_in, g_ss, g_rs)
-    stages = [(d, flip(m, b)) for b in mp_bits] + [(flip(d, b), m) for b in dp_bits]
-
-    def loss_copy(i):
-        return copy(lsum.at[i], lin.at[i], l_ss.at[i], l_rs.at[i], stages[i])
+    stages = []
+    for bits, peer in ((mp_bits, lambda o: (d, flip_all(m, o))), (dp_bits, lambda o: (flip_all(d, o), m))):
+        for i in range(0, len(bits), 2):
+            pair = bits[i:i + 2]
+            stages.append([peer(sum(pair[:1]))] if len(pair) == 1 else [peer(o) for o in (*pair, sum(pair))])
+
+    def loss_copies(i):
+        return [copy(lsum.at[i], lin.at[i, j], l_ss.at[i, j], l_rs.at[i, j], dev) for j, dev in enumerate(stages[i])]
 
     def loss_step(i):
-        if i > len(stages):
-            return
         if i:
-            loss_copy(i - 1).wait_recv()
-            lsum[i] = lsum[i - 1] + lin[i - 1]
+            for j, c in enumerate(loss_copies(i - 1)):
+                c.wait_recv()
+            lsum[i] = functools.reduce(lambda x, y: x + y, [lin[i - 1, j] for j in range(len(stages[i - 1]))], lsum[i - 1])
         if i < len(stages):
-            loss_copy(i).start()
+            for c in loss_copies(i):
+                c.start()
 
     local.begin()
     loss_step(0)
-    for c in range(1, first):
+    for c in range(1, CHUNKS):
         qs.relay(c)
-        loss_step(c)
     for k in range(1, WIN + 1):
         dispatch(k).wait_recv()
     foreign.begin()
-    for c in range(first, CHUNKS):
-        qs.relay(c)
-        loss_step(c)
     local.rest()
+    loss_step(1)
     local.all()
 
     @pl.loop(0, nmp)
@@ -386,10 +408,6 @@
 
     foreign.rest()
     foreign.all()
-    for i in range(CHUNKS, len(stages) + 1):
-        loss_step(i)
-    total_count = functools.reduce(lambda x, y: x + y, [counts_ref[i] for i in range(ndp)])
-    loss_ref[...] = lsum[len(stages), 0:1, 0:1] / total_count.astype(jnp.float32)
 
     def back(w, x):
         return lax.dot_general(w, x, COLS_BY_ROWS, preferred_element_type=jnp.float32)
@@ -397,29 +415,32 @@
     qs.early()
     far = 1 - parity
     mid = (1 + far, half_of(1 - far))
-    late_a = (2 - far, half_of(1))
-    late_b = (2, half_of(far))
+    late_a = (2 - far, half_of(far))
 
     for r in range(2):
         at = pl.ds(r * half, half)
         acc[at, :] = (back(weights[WIN + 1, :, at], q_ref[...]) + back(rw_in[0, :, at], qbuf[0])
                       + back(rw_in[1, 0:half, at], qbuf[1, 0:half, :])
                       + back(rw_in[mid[0], mid[1], at], qbuf[mid[0], mid[1], :]))
+    for i in range(2, len(stages)):
+        loss_step(i)
     for c in range(first, CHUNKS):
         qs.relay_late(c)
+    qs.late()
     for r in range(2):
         at = pl.ds(r * half, half)
         acc[at, :] = acc[at, :] + back(rw_in[late_a[0], late_a[1], at], qbuf[late_a[0], late_a[1], :])
-    qs.late()
+    loss_step(len(stages))
+    total_count = functools.reduce(lambda x, y: x + y, [counts_ref[i] for i in range(ndp)])
+    loss_ref[...] = lsum[len(stages), 0:1, 0:1] / total_count.astype(jnp.float32)
+    qs.last()
     for r in range(2):
         at = pl.ds(r * half, half)
-        gp_ref[at, :] = (acc[at, :] + back(rw_in[late_b[0], late_b[1], at], qbuf[late_b[0], late_b[1], :])
-                         ).astype(jnp.bfloat16)
+        gp_ref[at, :] = (acc[at, :] + back(rw_in[2, half:rows, at], qbuf[2, half:rows, :])).astype(jnp.bfloat16)
 
     ps.finish()
     qs.finish()
     for k in range(1, WIN + 1):
-        scale_copy(k).wait_send()
         dispatch(k).wait_send()
     for k in range(WIN + 1):
         for h in range(2):
@@ -428,19 +449,19 @@
     local.finish()
     foreign.finish()
     for i in range(len(stages)):
-        loss_copy(i).wait_send()
+        for c in loss_copies(i):
+            c.wait_send()
 
 
 def local(ndp, nmp, query, passage, query_scale, passage_scale, partners, counts):
     rows, width = query.shape
     inv = 1.0 / math.sqrt(width * nmp)
     share = rows // nmp
-    nst = (ndp * nmp).bit_length() - 1
+    nst = sum(n.bit_length() // 2 for n in (ndp, nmp))
     bf, f32 = jnp.bfloat16, jnp.float32
     dma = pltpu.SemaphoreType.DMA
     vm = pl.BlockSpec(memory_space=pltpu.VMEM)
-    sm = pl.BlockSpec(memory_space=pltpu.SMEM)
-    hbm = pl.BlockSpec(memory_space=pl.ANY)
+    hbm = pl.BlockSpec(memory_space=pltpu.HBM)
     gq, gp, loss = pl.pallas_call(
         functools.partial(kernel, ndp, nmp, inv),
         out_shape=[
@@ -448,11 +469,15 @@
             jax.ShapeDtypeStruct((rows, width), bf),
             jax.ShapeDtypeStruct((1, 1), f32),
         ],
-        in_specs=[hbm, hbm, vm, vm, sm, sm],
+        in_specs=[hbm] * 6,
         out_specs=[vm] * 3,
         scratch_shapes=[
             pltpu.VMEM((rows, width), bf),
             pltpu.VMEM((rows, width), bf),
+            pltpu.VMEM((rows,), bf),
+            pltpu.VMEM((rows,), bf),
+            pltpu.SMEM(partners.shape, jnp.int32),
+            pltpu.SMEM(counts.shape, jnp.int32),
             pltpu.VMEM((WIN, rows, width), bf),
             pltpu.VMEM((WIN, rows, width), bf),
             pltpu.VMEM((8, rows), f32),
@@ -464,20 +489,20 @@
             pltpu.VMEM((WIN, rows, rows), bf),
             pltpu.VMEM((rows, width), f32),
             pltpu.VMEM((nst + 1, 8, 128), f32),
-            pltpu.VMEM((nst, 8, 128), f32),
-            dma((2,)),
-            dma((4, CHUNKS)), dma((WIN, CHUNKS)),
-            dma((4, CHUNKS)), dma((WIN, CHUNKS)),
-            dma((WIN,)), dma((WIN,)),
+            pltpu.VMEM((nst, 3, 8, 128), f32),
+            dma((6,)),
+            dma((4, CHUNKS + 1)), dma((WIN, CHUNKS + 1)),
+            dma((4, CHUNKS + 1)), dma((WIN, CHUNKS + 1)),
             dma((nmp - 1, WIN + 1, 2)), dma((nmp - 1, WIN + 1, 2)),
             dma((nmp,)), dma((nmp,)),
             dma((WIN,)), dma((WIN,)),
             dma((nmp,)), dma((nmp,)),
-            dma((nst,)), dma((nst,)),
+            dma((nst, 3)), dma((nst, 3)),
         ],
         compiler_params=pltpu.CompilerParams(
             collective_id=0, has_side_effects=True, vmem_limit_bytes=48 * 1024 * 1024),
-    )(query, passage, passage_scale[None, :], query_scale[None, :], partners, counts)
+    )(*[pltpu.with_memory_space_constraint(x, pltpu.HBM)
+        for x in (query, passage, passage_scale, query_scale, partners, counts)])
     return loss.reshape(()), gq, gp
 
 

time: 124 us -> 111 us (0.90)
  Pallas kernels: 116 us -> 107 us
  local copies, waits for them, and re-layouts: 5.74 us -> 1.94 us
    pallas_call x1, Pallas kernels: 116 us -> 107 us  [local(): pl.pallas_call(functools.partial(kernel, ndp, nmp, inv), out_shape=[jax.S...]
    unnamed x12 -> x2, local copies, waits for them, and re-layouts: 5.05 us -> 1.94 us
where the time goes in v2:
time: 111 us
  Pallas kernels  107 us (96%)
  between operations  2.33 us (2%)
  local copies, waits for them, and re-layouts  1.94 us (2%)
    pallas_call x1, Pallas kernels, local(): pl.pallas_call(functools.partial(kernel, ndp, nmp, inv), out_shape=[jax.S...  107 us

profile of v2, /device:TPU:0, one launch (start us, length us, event | category | flops | bytes accessed | tf_op | source)
XLA Modules:
  0.0 111.1 jit_solution(393432604130699985)
XLA Ops:
  0.6 106.8 %shard_map.85 = (bf16[512,1024]{1,0:T(8,128)(2,1)S(1)}, bf16[512,1024]{1,0:T(8,128)(2,1)S(1)}, f32[1,1]{1,0:T(1,128)}) custom-call(bf16[512,1024]{1,0:T(8,128)(2,1)} %q_hbm.1, bf16[512,1024]{1,0:T(8,128)(2,1)} %p_hbm.1, bf16[512]{0:T(512)(128)(2,1)} %ps_hbm.1, bf16[512]{0:T(512)(128)(2,1)} %qs_hbm.1, s32[1,3]{1,0:T(1,128)} %partners_hbm.1, s32[8]{0:T(128)} %counts_hbm.1), custom_call_target="tpu_custom_call" | custom-call | tf_op jit(solution)/shard_map/pallas_call | solution.py:465
  108.0 1.0 copy.13
  109.0 1.0 copy.14

commit v3 on v2

--- a/solution.py
+++ b/solution.py
@@ -11,6 +11,7 @@
 WIN = 3
 CHUNKS = 8
 FIRST = 5
+AHEAD = 4
 GROUP = 32
 MESH = pl.DeviceIdType.MESH
 ROWS_BY_ROWS = (((1,), (1,)), ((), ()))
@@ -116,17 +117,30 @@
         def arrived(self, slot, c):
             self.move(0, slot, slot, c, partner).wait_recv()
 
-        def begin(self):
-            @pl.when(self.far)
-            def _():
-                for c in self.order:
+        def begin_direct(self, far, order):
+            @pl.when(self.far if far else self.near)
+            def _():
+                for c in order:
+                    if c < first or not far:
+                        self.direct(c).start()
+
+        def begin_across(self, order):
+            @pl.when(self.far)
+            def _():
+                for c in order:
+                    self.across_own(c).start()
+
+        def begin(self, order):
+            @pl.when(self.far)
+            def _():
+                for c in order:
                     self.across_own(c).start()
                     if c < first:
                         self.direct(c).start()
 
             @pl.when(self.near)
             def _():
-                for c in self.order:
+                for c in order:
                     self.direct(c).start()
 
         def relay(self, c):
@@ -204,7 +218,7 @@
     ps = Stream(p_hbm, pbuf, p_ss, p_rs, at_dp(-2), odd, (psown, psbuf))
     qs = Stream(q_hbm, qbuf, q_ss, q_rs, at_dp(2), even)
 
-    ps.begin()
+    ps.begin(ps.order)
 
     def across(s):
         block = m
@@ -252,14 +266,19 @@
     tile_next(1, 0)
     for c in range(middle + 2, CHUNKS):
         ps.relay(c)
+    qs.begin_direct(True, range(5))
     tile_far(1, 1)
     ps.early()
     tile_far(2 + parity, 1 - parity)
     tile_next(1, 1)
     tile_next(2 + parity, 1 - parity)
+    qs.begin_direct(False, range(0))
     for c in range(first, CHUNKS):
         ps.relay_late(c)
-    qs.begin()
+        if c == first: qs.begin_direct(False, range(0, 2))
+    qs.begin_across(range(CHUNKS))
+    qs.begin_direct(False, range(2,CHUNKS))
+    qs.begin_direct(True, range(5,CHUNKS))
     ps.late()
     tile_far(3 - parity, parity)
     ps.last()
@@ -267,7 +286,8 @@
     tile_next(3 - parity, parity)
     tile_next(3, 1)
     ps.last_extra()
-    qs.relay(0)
+    for c in range(2):
+        qs.relay(c)
     for c in small[1:]:
         c.wait()
     for k in range(WIN + 1):
@@ -324,12 +344,12 @@
     def dispatch(k):
         return copy(rw_out.at[k - 1], rw_in.at[k - 1, rows_of(m)], d_ss.at[k - 1], d_rs.at[k - 1], at_dp(k))
 
-    for k in range(1, WIN + 1):
+    for k in (2, 3, 1):
         dispatch(k).start()
 
     class Gather:
-        def __init__(self, buf, ss, rs):
-            self.buf, self.ss, self.rs = buf, ss, rs
+        def __init__(self, part, ss, rs):
+            self.part, self.ss, self.rs = part, ss, rs
             known = [0]
             self.steps = []
             for bit in reversed(mp_bits):
@@ -339,13 +359,13 @@
             self.got = set()
 
         def hop(self, s, bit):
-            part = self.buf.at[:, across(s)]
+            part = self.part(s)
             return copy(part, part, self.ss.at[s ^ bit], self.rs.at[s ^ bit], (d, flip(m, bit)))
 
         def take(self, s):
             if s and s not in self.got:
                 self.got.add(s)
-                part = self.buf.at[:, across(s)]
+                part = self.part(s)
                 copy(part, part, self.ss.at[s], self.rs.at[s], (d, flip(m, 1))).wait_recv()
 
         def begin(self):
@@ -367,8 +387,9 @@
             for s, bit in self.steps:
                 self.hop(s, bit).wait_send()
 
-    local = Gather(weights, k_ss, k_rs)
-    foreign = Gather(rw_in, g_ss, g_rs)
+    local = Gather(lambda s: weights.at[:, across(s)], k_ss, k_rs)
+    foreign = {k: Gather(lambda s, k=k: rw_in.at[k - 1, across(s)], g_ss.at[k - 1], g_rs.at[k - 1])
+               for k in range(1, WIN + 1)}
     stages = []
     for bits, peer in ((mp_bits, lambda o: (d, flip_all(m, o))), (dp_bits, lambda o: (flip_all(d, o), m))):
         for i in range(0, len(bits), 2):
@@ -389,54 +410,71 @@
 
     local.begin()
     loss_step(0)
-    for c in range(1, CHUNKS):
-        qs.relay(c)
-    for k in range(1, WIN + 1):
-        dispatch(k).wait_recv()
-    foreign.begin()
-    local.rest()
-    loss_step(1)
-    local.all()
-
-    @pl.loop(0, nmp)
-    def _(r):
+
+    def back(w, x):
+        return lax.dot_general(w, x, COLS_BY_ROWS, preferred_element_type=jnp.float32)
+
+    far = 1 - parity
+    mid = (1 + far, half_of(1 - far))
+    late = (2 - far, half_of(far))
+
+    def grad_query(r):
         at = rows_of(r)
         out = jnp.dot(weights[0, at, :], p_ref[...], preferred_element_type=jnp.float32)
         for k in range(WIN):
             out = out + jnp.dot(weights[k + 1, at, :], pbuf[k], preferred_element_type=jnp.float32)
         gq_ref[at, :] = out.astype(jnp.bfloat16)
 
-    foreign.rest()
-    foreign.all()
-
-    def back(w, x):
-        return lax.dot_general(w, x, COLS_BY_ROWS, preferred_element_type=jnp.float32)
-
-    qs.early()
-    far = 1 - parity
-    mid = (1 + far, half_of(1 - far))
-    late_a = (2 - far, half_of(far))
-
-    for r in range(2):
-        at = pl.ds(r * half, half)
-        acc[at, :] = (back(weights[WIN + 1, :, at], q_ref[...]) + back(rw_in[0, :, at], qbuf[0])
-                      + back(rw_in[1, 0:half, at], qbuf[1, 0:half, :])
-                      + back(rw_in[mid[0], mid[1], at], qbuf[mid[0], mid[1], :]))
+    def grad_passage(terms, start, end):
+        for r in range(2):
+            at = pl.ds(r * half, half)
+            out = [back(w[:, at], x) for w, x in terms()]
+            out = functools.reduce(lambda x, y: x + y, out)
+            if not start:
+                out = acc[at, :] + out
+            if end:
+                gp_ref[at, :] = out.astype(jnp.bfloat16)
+            else:
+                acc[at, :] = out
+
+    def piece(slot, at):
+        return rw_in.at[slot, at], qbuf[slot, at, :]
+
+    def foreign_begin(k):
+        dispatch(k).wait_recv()
+        foreign[k].begin()
+
+    for c in range(2, CHUNKS):
+        qs.relay(c)
+        if c == middle:
+            loss_step(1)
+    for k in (2, 1, 3):
+        foreign_begin(k)
+    local.rest()
+    qs.relay_late(first)
+    local.all()
+    for r in range(nmp):
+        grad_query(r)
+        if r == 1:
+            qs.relay_late(first + 1)
+    for c in range(first + 2, CHUNKS):
+        qs.relay_late(c)
+    grad_passage(lambda: [(weights.at[WIN + 1], q_ref[...])], True, False)
     for i in range(2, len(stages)):
         loss_step(i)
-    for c in range(first, CHUNKS):
-        qs.relay_late(c)
+    for k in (2, 1, 3):
+        foreign[k].rest()
+    for k in (2, 1, 3):
+        foreign[k].all()
+    qs.early()
+    grad_passage(lambda: [piece(0, half_of(0)), piece(0, half_of(1)), piece(1, half_of(0)), piece(*mid)], False, False)
     qs.late()
-    for r in range(2):
-        at = pl.ds(r * half, half)
-        acc[at, :] = acc[at, :] + back(rw_in[late_a[0], late_a[1], at], qbuf[late_a[0], late_a[1], :])
+    grad_passage(lambda: [piece(*late)], False, False)
     loss_step(len(stages))
     total_count = functools.reduce(lambda x, y: x + y, [counts_ref[i] for i in range(ndp)])
     loss_ref[...] = lsum[len(stages), 0:1, 0:1] / total_count.astype(jnp.float32)
     qs.last()
-    for r in range(2):
-        at = pl.ds(r * half, half)
-        gp_ref[at, :] = (acc[at, :] + back(rw_in[2, half:rows, at], qbuf[2, half:rows, :])).astype(jnp.bfloat16)
+    grad_passage(lambda: [piece(2, half_of(1))], False, True)
 
     ps.finish()
     qs.finish()
@@ -447,7 +485,8 @@
             for j in range(1, nmp):
                 tile_copy(k, h, j).wait_send()
     local.finish()
-    foreign.finish()
+    for k in range(1, WIN + 1):
+        foreign[k].finish()
     for i in range(len(stages)):
         for c in loss_copies(i):
             c.wait_send()
@@ -496,7 +535,7 @@
             dma((nmp - 1, WIN + 1, 2)), dma((nmp - 1, WIN + 1, 2)),
             dma((nmp,)), dma((nmp,)),
             dma((WIN,)), dma((WIN,)),
-            dma((nmp,)), dma((nmp,)),
+            dma((WIN, nmp)), dma((WIN, nmp)),
             dma((nst, 3)), dma((nst, 3)),
         ],
         compiler_params=pltpu.CompilerParams(

time: 111 us -> 106 us (0.955); the launches traced: 111 us -> 105 us
  Pallas kernels: 107 us -> 101 us
    pallas_call x1, Pallas kernels: 107 us -> 101 us  [local(): pl.pallas_call(functools.partial(kernel, ndp, nmp, inv), out_shape=[jax.S...]
where the time goes in v3:
time: 106 us; the launch traced here: 105 us
  Pallas kernels  101 us (95%)
  between operations  2.33 us (2%)
  local copies, waits for them, and re-layouts  1.94 us (2%)
    pallas_call x1, Pallas kernels, local(): pl.pallas_call(functools.partial(kernel, ndp, nmp, inv), out_shape=[jax.S...  101 us

profile of v3, /device:TPU:0, one launch (start us, length us, event | category | flops | bytes accessed | tf_op | source)
XLA Modules:
  0.0 104.9 jit_solution(289893922433272978)
XLA Ops:
  0.6 100.6 %shard_map.85 = (bf16[512,1024]{1,0:T(8,128)(2,1)S(1)}, bf16[512,1024]{1,0:T(8,128)(2,1)S(1)}, f32[1,1]{1,0:T(1,128)}) custom-call(bf16[512,1024]{1,0:T(8,128)(2,1)} %q_hbm.1, bf16[512,1024]{1,0:T(8,128)(2,1)} %p_hbm.1, bf16[512]{0:T(512)(128)(2,1)} %ps_hbm.1, bf16[512]{0:T(512)(128)(2,1)} %qs_hbm.1, s32[1,3]{1,0:T(1,128)} %partners_hbm.1, s32[8]{0:T(128)} %counts_hbm.1), custom_call_target="tpu_custom_call" | custom-call | tf_op jit(solution)/shard_map/pallas_call | solution.py:504
  101.8 1.0 copy.13
  102.8 1.0 copy.14

commit v4 on v3

--- a/solution.py
+++ b/solution.py
@@ -11,7 +11,8 @@
 WIN = 3
 CHUNKS = 8
 FIRST = 5
-AHEAD = 4
+FIRST_Q = 6
+AHEAD = 6
 GROUP = 32
 MESH = pl.DeviceIdType.MESH
 ROWS_BY_ROWS = (((1,), (1,)), ((), ()))
@@ -82,9 +83,9 @@
             device_id=dev, device_id_type=MESH)
 
     class Stream:
-        def __init__(self, own, buf, ss, rs, dest, far, extra=None):
+        def __init__(self, own, buf, ss, rs, dest, far, first, extra=None):
             self.own, self.buf, self.ss, self.rs, self.dest = own, buf, ss, rs, dest
-            self.far, self.near, self.extra = far, jnp.logical_not(far), extra
+            self.far, self.near, self.extra, self.first = far, jnp.logical_not(far), extra, first
             self.order = ([] if extra is None else [-1]) + list(range(CHUNKS))
 
         def cut(self, slot, c):
@@ -121,7 +122,7 @@
             @pl.when(self.far if far else self.near)
             def _():
                 for c in order:
-                    if c < first or not far:
+                    if c < self.first or not far:
                         self.direct(c).start()
 
         def begin_across(self, order):
@@ -135,7 +136,7 @@
             def _():
                 for c in order:
                     self.across_own(c).start()
-                    if c < first:
+                    if c < self.first:
                         self.direct(c).start()
 
             @pl.when(self.near)
@@ -146,7 +147,7 @@
         def relay(self, c):
             @pl.when(self.far)
             def _():
-                if c < first:
+                if c < self.first:
                     self.arrived(1, c)
                     self.across_first(c).start()
                 self.arrived(0, c)
@@ -157,7 +158,7 @@
                 self.arrived(1, c)
                 self.across_one(c).start()
                 self.arrived(0, c)
-                if c >= first:
+                if c >= self.first:
                     self.onward(c).start()
 
         def early(self):
@@ -179,7 +180,7 @@
         def late(self):
             @pl.when(self.near)
             def _():
-                for c in range(middle):
+                for c in range(min(middle, self.first)):
                     self.arrived(2, c)
 
         def last(self):
@@ -190,7 +191,7 @@
 
             @pl.when(self.near)
             def _():
-                for c in range(middle, first):
+                for c in range(middle, self.first):
                     self.arrived(2, c)
 
         def last_extra(self):
@@ -202,7 +203,7 @@
                 for c in self.order:
                     self.across_own(c).wait_send()
                     self.onward(c).wait_send()
-                    if c < first:
+                    if c < self.first:
                         self.direct(c).wait_send()
                         self.across_first(c).wait_send()
 
@@ -211,14 +212,15 @@
                 for c in self.order:
                     self.direct(c).wait_send()
                     self.across_one(c).wait_send()
-                    if c >= first:
+                    if c >= self.first:
                         self.onward(c).wait_send()
                         self.across_second(c).wait_send()
 
-    ps = Stream(p_hbm, pbuf, p_ss, p_rs, at_dp(-2), odd, (psown, psbuf))
-    qs = Stream(q_hbm, qbuf, q_ss, q_rs, at_dp(2), even)
+    ps = Stream(p_hbm, pbuf, p_ss, p_rs, at_dp(-2), odd, FIRST, (psown, psbuf))
+    qs = Stream(q_hbm, qbuf, q_ss, q_rs, at_dp(2), even, FIRST_Q)
 
     ps.begin(ps.order)
+    qs.begin_across(range(2))
 
     def across(s):
         block = m
@@ -266,19 +268,17 @@
     tile_next(1, 0)
     for c in range(middle + 2, CHUNKS):
         ps.relay(c)
-    qs.begin_direct(True, range(5))
+    qs.begin_direct(True, range(FIRST_Q))
     tile_far(1, 1)
     ps.early()
     tile_far(2 + parity, 1 - parity)
     tile_next(1, 1)
     tile_next(2 + parity, 1 - parity)
-    qs.begin_direct(False, range(0))
     for c in range(first, CHUNKS):
         ps.relay_late(c)
         if c == first: qs.begin_direct(False, range(0, 2))
-    qs.begin_across(range(CHUNKS))
-    qs.begin_direct(False, range(2,CHUNKS))
-    qs.begin_direct(True, range(5,CHUNKS))
+    qs.begin_across(range(2, CHUNKS))
+    qs.begin_direct(False, range(2, AHEAD))
     ps.late()
     tile_far(3 - parity, parity)
     ps.last()
@@ -387,7 +387,8 @@
             for s, bit in self.steps:
                 self.hop(s, bit).wait_send()
 
-    local = Gather(lambda s: weights.at[:, across(s)], k_ss, k_rs)
+    local = Gather(lambda s: weights.at[0:WIN + 1, across(s)], k_ss.at[0], k_rs.at[0])
+    local_rows = Gather(lambda s: weights.at[WIN + 1, across(s)], k_ss.at[1], k_rs.at[1])
     foreign = {k: Gather(lambda s, k=k: rw_in.at[k - 1, across(s)], g_ss.at[k - 1], g_rs.at[k - 1])
                for k in range(1, WIN + 1)}
     stages = []
@@ -408,7 +409,9 @@
             for c in loss_copies(i):
                 c.start()
 
+    qs.begin_direct(False, range(AHEAD, CHUNKS))
     local.begin()
+    local_rows.begin()
     loss_step(0)
 
     def back(w, x):
@@ -451,14 +454,18 @@
     for k in (2, 1, 3):
         foreign_begin(k)
     local.rest()
-    qs.relay_late(first)
+    if FIRST_Q <= first:
+        qs.relay_late(first)
     local.all()
+    local_rows.rest()
     for r in range(nmp):
         grad_query(r)
         if r == 1:
-            qs.relay_late(first + 1)
-    for c in range(first + 2, CHUNKS):
+            if FIRST_Q <= first + 1:
+                qs.relay_late(first + 1)
+    for c in range(max(FIRST_Q, first + 2), CHUNKS):
         qs.relay_late(c)
+    local_rows.all()
     grad_passage(lambda: [(weights.at[WIN + 1], q_ref[...])], True, False)
     for i in range(2, len(stages)):
         loss_step(i)
@@ -485,6 +492,7 @@
             for j in range(1, nmp):
                 tile_copy(k, h, j).wait_send()
     local.finish()
+    local_rows.finish()
     for k in range(1, WIN + 1):
         foreign[k].finish()
     for i in range(len(stages)):
@@ -533,7 +541,7 @@
             dma((4, CHUNKS + 1)), dma((WIN, CHUNKS + 1)),
             dma((4, CHUNKS + 1)), dma((WIN, CHUNKS + 1)),
             dma((nmp - 1, WIN + 1, 2)), dma((nmp - 1, WIN + 1, 2)),
-            dma((nmp,)), dma((nmp,)),
+            dma((2, nmp)), dma((2, nmp)),
             dma((WIN,)), dma((WIN,)),
             dma((WIN, nmp)), dma((WIN, nmp)),
             dma((nst, 3)), dma((nst, 3)),

time: 106 us -> 102 us (0.962)
  Pallas kernels: 101 us -> 96.9 us
    pallas_call x1, Pallas kernels: 101 us -> 96.9 us  [local(): pl.pallas_call(functools.partial(kernel, ndp, nmp, inv), out_shape=[jax.S...]
where the time goes in v4:
time: 102 us; the launch traced here: 101 us
  Pallas kernels  96.9 us (95%)
  between operations  2.33 us (2%)
  local copies, waits for them, and re-layouts  1.94 us (2%)
    pallas_call x1, Pallas kernels, local(): pl.pallas_call(functools.partial(kernel, ndp, nmp, inv), out_shape=[jax.S...  96.9 us

profile of v4, /device:TPU:0, one launch (start us, length us, event | category | flops | bytes accessed | tf_op | source)
XLA Modules:
  0.0 101.1 jit_solution(15998551436631509354)
XLA Ops:
  0.6 96.9 %shard_map.85 = (bf16[512,1024]{1,0:T(8,128)(2,1)S(1)}, bf16[512,1024]{1,0:T(8,128)(2,1)S(1)}, f32[1,1]{1,0:T(1,128)}) custom-call(bf16[512,1024]{1,0:T(8,128)(2,1)} %q_hbm.1, bf16[512,1024]{1,0:T(8,128)(2,1)} %p_hbm.1, bf16[512]{0:T(512)(128)(2,1)} %ps_hbm.1, bf16[512]{0:T(512)(128)(2,1)} %qs_hbm.1, s32[1,3]{1,0:T(1,128)} %partners_hbm.1, s32[8]{0:T(128)} %counts_hbm.1), custom_call_target="tpu_custom_call" | custom-call | tf_op jit(solution)/shard_map/pallas_call | solution.py:512
  98.1 1.0 copy.13
  99.0 1.0 copy.14

commit v5 on v4

--- a/solution.py
+++ b/solution.py
@@ -451,7 +451,9 @@
         qs.relay(c)
         if c == middle:
             loss_step(1)
-    for k in (2, 1, 3):
+        if c == CHUNKS - 2:
+            foreign_begin(2)
+    for k in (1, 3):
         foreign_begin(k)
     local.rest()
     if FIRST_Q <= first:

time: 102 us -> 101 us (level)
  no operation moved by 1% of the time
where the time goes in v5:
time: 101 us
  Pallas kernels  96.7 us (96%)
  between operations  2.33 us (2%)
  local copies, waits for them, and re-layouts  1.94 us (2%)
    pallas_call x1, Pallas kernels, local(): pl.pallas_call(functools.partial(kernel, ndp, nmp, inv), out_shape=[jax.S...  96.7 us

profile of v5, /device:TPU:0, one launch (start us, length us, event | category | flops | bytes accessed | tf_op | source)
XLA Modules:
  0.0 100.9 jit_solution(16045728111391746831)
XLA Ops:
  0.6 96.7 %shard_map.85 = (bf16[512,1024]{1,0:T(8,128)(2,1)S(1)}, bf16[512,1024]{1,0:T(8,128)(2,1)S(1)}, f32[1,1]{1,0:T(1,128)}) custom-call(bf16[512,1024]{1,0:T(8,128)(2,1)} %q_hbm.1, bf16[512,1024]{1,0:T(8,128)(2,1)} %p_hbm.1, bf16[512]{0:T(512)(128)(2,1)} %ps_hbm.1, bf16[512]{0:T(512)(128)(2,1)} %qs_hbm.1, s32[1,3]{1,0:T(1,128)} %partners_hbm.1, s32[8]{0:T(128)} %counts_hbm.1), custom_call_target="tpu_custom_call" | custom-call | tf_op jit(solution)/shard_map/pallas_call | solution.py:514
  97.9 1.0 copy.13
  98.8 1.0 copy.14

commit v6 on v5

--- a/solution.py
+++ b/solution.py
@@ -65,7 +65,8 @@
 
     peers = [partner, at_dp(2), at_dp(-2)]
     peers += [(d, flip(m, b)) for b in mp_bits]
-    peers += [(flip(d, b), m) for b in dp_bits if b > WIN + 1]
+    jumps = {sum(c) for i in range(0, len(dp_bits), 2) for c in (dp_bits[i:i + 1], dp_bits[i + 1:i + 2], dp_bits[i:i + 2])}
+    peers += [(flip_all(d, o), m) for o in sorted(jumps) if o > WIN + 1]
     barrier = pltpu.get_barrier_semaphore()
     for peer in peers:
         pl.semaphore_signal(barrier, inc=1, device_id=peer, device_id_type=MESH)

time: 101 us -> 101 us (level)
  no operation moved by 1% of the time
where the time goes in v6:
time: 101 us
  Pallas kernels  96.7 us (96%)
  between operations  2.33 us (2%)
  local copies, waits for them, and re-layouts  1.94 us (2%)
    pallas_call x1, Pallas kernels, local(): pl.pallas_call(functools.partial(kernel, ndp, nmp, inv), out_shape=[jax.S...  96.7 us

profile of v6, /device:TPU:0, one launch (start us, length us, event | category | flops | bytes accessed | tf_op | source)
XLA Modules:
  0.0 100.9 jit_solution(16045728111391746831)
XLA Ops:
  0.6 96.7 %shard_map.85 = (bf16[512,1024]{1,0:T(8,128)(2,1)S(1)}, bf16[512,1024]{1,0:T(8,128)(2,1)S(1)}, f32[1,1]{1,0:T(1,128)}) custom-call(bf16[512,1024]{1,0:T(8,128)(2,1)} %q_hbm.1, bf16[512,1024]{1,0:T(8,128)(2,1)} %p_hbm.1, bf16[512]{0:T(512)(128)(2,1)} %ps_hbm.1, bf16[512]{0:T(512)(128)(2,1)} %qs_hbm.1, s32[1,3]{1,0:T(1,128)} %partners_hbm.1, s32[8]{0:T(128)} %counts_hbm.1), custom_call_target="tpu_custom_call" | custom-call | tf_op jit(solution)/shard_map/pallas_call | solution.py:515
  97.9 1.0 copy.13
  98.8 1.0 copy.14
